TPU v7x, 256 devices: a whole 4x4x8 slice. The times are simulated.
256 devices in a mesh: dp: 8 (over z), ctx: 32 (over y, x, core).
Axes of the slice: x: 4, y: 4, z: 8, core: 2. Of those that a mesh axis runs over, the one named last changes fastest.
Arguments:
- queries: bfloat16 [8, 4096, 2048], P('dp', 'ctx'), may hold values from -6 to 6
- keys: bfloat16 [8, 4096, 2048], P('dp', 'ctx'), may hold values from -6 to 6
- values: bfloat16 [8, 4096, 2048], P('dp', 'ctx'), may hold values from -6 to 6
- grad_output: bfloat16 [8, 4096, 2048], P('dp', 'ctx'), may hold values from -6 to 6
- out_gain: float32 [2048], replicated, may hold values from 0.5 to 1.5
- doc_lengths: int32 [8, 12], P('dp'), may hold values from 1 to 1365, 4096 in all within a row
Outputs:
- output: bfloat16 [8, 4096, 2048], P('dp', 'ctx')
- grad_queries: bfloat16 [8, 4096, 2048], P('dp', 'ctx')
- grad_keys: bfloat16 [8, 4096, 2048], P('dp', 'ctx')
- grad_values: bfloat16 [8, 4096, 2048], P('dp', 'ctx')
- grad_gain: float32 [2048], replicated
Inputs may be any that keep to these rules, and one draw needn't show every extreme that they name: `doc_lengths`: each row holds the lengths of 12 documents packed end to end; they sum to 4096, and the largest is exactly 1365.
All inputs are finite; a program needn't handle non-finite values.
Results may differ from a plain program's by a relative error of at most 0.012.
The roundings to bfloat16 on the way count: a program that leaves them out, or rounds other values in their place, can miss the bound.
Values may be sent and summed in bfloat16 or wider, within the bound.
No kernel may reach another device: no remote copies, remote signals or barrier semaphores. Data moves between devices by JAX's collectives and lax.ppermute only.
A program may use at most 64 MiB of HBM per device.

v0:
```python
import math
import jax
import jax.numpy as jnp
from jax import lax
from jax.sharding import PartitionSpec as P

H = 32
E = 64
eps = 1e-05


def entering(part, axis, combine, identity):
    place = lax.axis_index(axis)
    gathered = jax.tree.map(lambda a: lax.all_gather(a, axis), part)
    state = jax.tree.map(lambda a, e: jnp.zeros_like(a) + jnp.asarray(e, a.dtype), part, identity)

    def entering_one(step, state):
        return combine(
            state, jax.tree.map(lambda a: lax.dynamic_index_in_dim(a, step, 0, False), gathered)
        )

    return lax.fori_loop(0, place, entering_one, state)


def carried_in(shard, axis, join, neutral):
    count = lax.axis_size(axis)
    place = lax.axis_index(axis)
    ahead = count - 1 - place
    gathered = jax.tree.map(
        lambda a, kind: lax.all_gather(a.astype(kind), axis), shard, (jnp.bfloat16, jnp.bfloat16)
    )
    state = jax.tree.map(lambda a, e: jnp.zeros_like(a) + jnp.asarray(e, a.dtype), shard, neutral)

    def carried_one(step, state):
        source = count - 1 - step
        return join(
            state,
            jax.tree.map(
                lambda a, own: lax.dynamic_index_in_dim(a, source, 0, False).astype(own.dtype),
                gathered,
                shard,
            ),
        )

    return lax.fori_loop(0, ahead, carried_one, state)


def doc_geometry(doc_lengths, positions):
    doc_ends = jnp.cumsum(doc_lengths, axis=1)
    begins = doc_ends - doc_lengths
    doc_ids = jnp.sum((positions[None, :, None] >= doc_ends[:, None, :]).astype(jnp.int32), axis=2)
    starts = jnp.sum((positions[None, :, None] == begins[:, None, :]).astype(jnp.float32), axis=2)
    return (doc_ids, starts)


def chain_join(earlier, later):
    keep = (1.0 - later[1]).reshape((-1,) + (1,) * (later[0].ndim - 1))
    state_sum = later[0] + keep * earlier[0]
    return (state_sum, jnp.maximum(earlier[1], later[1]))


def split_product(form, data, state):
    high_part = state.astype(jnp.bfloat16)
    low_part = (state - lax.optimization_barrier(high_part).astype(jnp.float32)).astype(
        jnp.bfloat16
    )
    first = jnp.einsum(form, data, high_part, preferred_element_type=jnp.float32)
    return first + jnp.einsum(form, data, low_part, preferred_element_type=jnp.float32)


def blocks_math(
    queries, keys, values, grad_output, gain_heads, doc_ids, starts, forward_carry, backward_carry
):
    counted = jnp.cumsum(starts, axis=1)
    totals = counted[:, -1:]
    before = (counted == 0).astype(jnp.float32)[:, :, None, None]
    after_mask = (totals - counted == 0).astype(jnp.float32)[:, :, None, None]
    opened = jnp.minimum(totals[:, 0], 1.0)
    row_ids = jnp.arange(queries.shape[1])
    causal = row_ids[:, None] >= row_ids[None, :]
    doc_mask = jnp.logical_and(causal[None], doc_ids[:, :, None] == doc_ids[:, None, :]).astype(
        jnp.float32
    )[:, None]
    scores = jnp.einsum("btge,bsge->bgts", queries, keys, preferred_element_type=jnp.float32)
    weights = (scores * doc_mask).astype(jnp.bfloat16)
    own_state = jnp.einsum(
        "bsge,bsgf->bgef",
        keys * after_mask.astype(jnp.bfloat16),
        values,
        preferred_element_type=jnp.float32,
    )
    carried = forward_carry(own_state, opened)
    attended = jnp.einsum("bgts,bsgf->btgf", weights, values, preferred_element_type=jnp.float32)
    attended = attended + before * split_product("btge,bgef->btgf", queries, carried)
    root_mean = jnp.sqrt(jnp.mean(attended * attended, axis=-1, keepdims=True) + eps)
    normed = attended / root_mean
    output = (gain_heads * normed).astype(jnp.bfloat16)
    dyf = grad_output.astype(jnp.float32)
    dnormed = dyf * gain_heads
    grad_att = (
        (dnormed - normed * jnp.mean(dnormed * normed, axis=-1, keepdims=True)) / root_mean
    ).astype(jnp.bfloat16)
    gain_part = jnp.sum(dyf * normed, axis=(0, 1))
    grad_scores = jnp.einsum(
        "btgf,bsgf->bgts", grad_att, values, preferred_element_type=jnp.float32
    )
    grad_weights = (grad_scores * doc_mask).astype(jnp.bfloat16)
    back_state = jnp.einsum(
        "btge,btgf->bgef",
        queries * before.astype(jnp.bfloat16),
        grad_att,
        preferred_element_type=jnp.float32,
    )
    back_carried = backward_carry(back_state, opened)
    grad_q = jnp.einsum("bgts,bsge->btge", grad_weights, keys, preferred_element_type=jnp.float32)
    grad_q = grad_q + before * split_product("btgf,bgef->btge", grad_att, carried)
    grad_k = jnp.einsum(
        "bgts,btge->bsge", grad_weights, queries, preferred_element_type=jnp.float32
    )
    grad_k = grad_k + after_mask * split_product("bsgf,bgef->bsge", values, back_carried)
    grad_v = jnp.einsum("bgts,btgf->bsgf", weights, grad_att, preferred_element_type=jnp.float32)
    grad_v = grad_v + after_mask * split_product("bsge,bgef->bsgf", keys, back_carried)
    return (
        output,
        grad_q.astype(jnp.bfloat16),
        grad_k.astype(jnp.bfloat16),
        grad_v.astype(jnp.bfloat16),
        gain_part,
    )


def per_device(queries, keys, values, grad_output, out_gain, doc_lengths):
    local_seqs, block_len, width = queries.shape
    ctx_count = lax.axis_size("ctx")
    ctx_index = lax.axis_index("ctx")
    shape4 = (local_seqs, block_len, H, E)
    quad = tuple((item.reshape(shape4) for item in (queries, keys, values, grad_output)))
    gain_heads = out_gain.reshape(H, E)
    positions = ctx_index * block_len + jnp.arange(block_len, dtype=jnp.int32)
    doc_ids, starts = doc_geometry(doc_lengths, positions)

    def chain_forward(state, opened):
        wide = state.reshape(state.shape[0], H, E * E)
        moved = entering(
            (wide, opened), "ctx", chain_join, (jnp.zeros_like(wide), jnp.zeros_like(opened))
        )[0]
        return moved.reshape(state.shape)

    def chain_backward(state, opened):
        wide = state.reshape(state.shape[0], H, E * E)
        moved = carried_in(
            (wide, opened), "ctx", chain_join, (jnp.zeros_like(wide), jnp.zeros_like(opened))
        )[0]
        return moved.reshape(state.shape)

    results = blocks_math(
        quad[0],
        quad[1],
        quad[2],
        quad[3],
        gain_heads,
        doc_ids,
        starts,
        chain_forward,
        chain_backward,
    )
    returned = results[:4]
    gain_terms = results[4]
    total_tokens = local_seqs * lax.axis_size("dp") * block_len * ctx_count
    grad_gain = lax.psum(gain_terms.reshape(H * E), ("dp", "ctx")) / math.sqrt(total_tokens)
    flat = (local_seqs, block_len, H * E)
    outputs = tuple((item.reshape(flat) for item in returned))
    return (outputs[0], outputs[1], outputs[2], outputs[3], grad_gain)


def solution(mesh):
    placed = (
        P("dp", "ctx", None),
        P("dp", "ctx", None),
        P("dp", "ctx", None),
        P("dp", "ctx", None),
        P(),
        P("dp", None),
    )
    return jax.shard_map(
        per_device,
        mesh=mesh,
        in_specs=placed,
        out_specs=(
            P("dp", "ctx", None),
            P("dp", "ctx", None),
            P("dp", "ctx", None),
            P("dp", "ctx", None),
            P(),
        ),
        check_vma=False,
    )
```

profile of v0, /device:TPU:32, one launch (start us, length us, event | category | flops | bytes accessed | tf_op | source)
XLA Modules:
  0.0 422.3 jit_solution(17803829553141644253)
XLA Ops:
  7.2 0.8 reduce_window_sum.22
  8.1 0.7 subtract_bitcast_fusion
  10.4 1.3 copy.66
  11.7 1.3 copy.67
  13.5 1.2 all_gather_reshape.3
  15.3 1.3 copy.65
  16.7 1.2 copy.70
  18.6 0.7 bitcast_dynamic-update-slice_fusion
  19.2 68.4 %all-reduce = f32[32]{0:T(128)S(1)} all-reduce(f32[32]{0:T(128)S(1)} %bitcast_dynamic-update-slice_fusion), channel_id=1, replica_groups=mesh['dp'=8,'ctx'=32] {'ctx'}, use_global_device_ids=true, to_apply=%add | all-reduce | flops 32 | bytes 256
  88.3 7.0 %all-gather.3.cloned.1.call-done = f32[32,1,32,4096]{3,2,1,0:T(8,128)} async-done(((f32[1,1,32,4096]{3,2,1,0:T(8,128)}), f32[32,1,32,4096]{3,2,1,0:T(8,128)}) %all-gather.3.cloned.1.call-update) | async-done | bytes 16777232 | tf_op jit(solution)/shard_map/all_gather | solution.py:14
  95.4 1.5 reshape.498
  97.8 0.9 copy-done
  99.5 0.8 multiply_reduce_fusion.2
  100.7 0.8 multiply_reduce_fusion
  101.6 1.3 divide_convert_fusion
  103.2 1.2 convert_element_type.251
  104.5 0.8 dynamic-update-slice.1
  105.2 143.0 %all-reduce.1 = bf16[32]{0:T(256)(128)(2,1)S(1)} all-reduce(bf16[32]{0:T(256)(128)(2,1)S(1)} %dynamic-update-slice.1), channel_id=1, replica_groups=mesh['dp'=8,'ctx'=32] {'ctx'}, use_global_device_ids=true, to_apply=%add.1 | all-reduce | flops 32 | bytes 128
  249.9 0.8 copy-done.4
  250.7 0.8 fusion.13
  251.5 1.0 copy.76
  252.5 1.0 copy.75
  253.6 73.1 %psum.7 = f32[2048]{0:T(1024)S(1)} all-reduce(f32[2048]{0:T(1024)S(1)} %reshape.507), channel_id=1, replica_groups=mesh['dp'=8,'ctx'=32] {'dp','ctx'}, use_global_device_ids=true, to_apply=%region_11.12 | all-reduce | flops 2048 | bytes 16384 | tf_op jit(solution)/shard_map/psum | solution.py:170
  327.3 74.7 %while.27 = (s32[]{:T(128)}, f32[1,32,4096]{2,1,0:T(8,128)S(1)}, s32[]{:T(128)}, bf16[32,1,32,4096]{3,2,1,0:T(8,128)(2,1)}, bf16[32,1]{0,1:T(2,128)(2,1)S(1)}, /*index=5*/s32[]{:T(128)}, s32[]{:T(128)}, s32[]{:T(128)}, s32[]{:T(128)}) while((s32[]{:T(128)}, f32[1,32,4096]{2,1,0:T(8,128)S(1)}, s32[]{:T(128)}, ...), condition=%wide.region_9.10_spmd, body=%wide.region_8.9_spmd.sunk | while | flops 393223 | bytes 1310877 | solution.py:45
  328.0 1.8 convert_add_fusion.2
  330.4 1.8 convert_add_fusion.2
  332.8 1.8 convert_add_fusion.2
  335.2 1.8 convert_add_fusion.2
  337.6 1.8 convert_add_fusion.2
  340.0 1.8 convert_add_fusion.2
  342.4 1.8 convert_add_fusion.2
  344.8 1.8 convert_add_fusion.2
  347.2 1.8 convert_add_fusion.2
  349.6 1.8 convert_add_fusion.2
  352.0 1.8 convert_add_fusion.2
  354.4 1.8 convert_add_fusion.2
  356.8 1.8 convert_add_fusion.2
  359.2 1.8 convert_add_fusion.2
  361.6 1.8 convert_add_fusion.2
  364.0 1.8 convert_add_fusion.2
  366.4 1.8 convert_add_fusion.2
  368.8 1.8 convert_add_fusion.2
  371.2 1.8 convert_add_fusion.2
  373.6 1.8 convert_add_fusion.2
  376.0 1.8 convert_add_fusion.2
  378.4 1.8 convert_add_fusion.2
  380.8 1.8 convert_add_fusion.2
  383.2 1.8 convert_add_fusion.2
  385.6 1.8 convert_add_fusion.2
  388.0 1.8 convert_add_fusion.2
  390.4 1.8 convert_add_fusion.2
  392.8 1.8 convert_add_fusion.2
  395.2 1.8 convert_add_fusion.2
  397.6 1.8 convert_add_fusion.2
  400.0 1.8 convert_add_fusion.2
  402.0 1.4 reshape.503
  404.0 1.3 fusion.46
  405.3 1.3 fusion.45
  406.6 1.6 copy.72
  408.3 1.3 copy-done.10
  409.9 0.9 copy-done.3
  411.2 1.0 copy.78
  412.2 1.8 fusion.11
  414.5 1.0 copy.77
  (97 shorter events, 28.5 us)
Async XLA Ops:
  7.2 88.1 %all-gather.3.cloned.1.call-start = ((), (), s32[]{:S(2)}) async-start(), calls=%async_computation | async-start | bytes 17301504 | tf_op jit(solution)/shard_map/all_gather | solution.py:14
  13.4 3.2 copy-start.12
  13.4 4.5 %copy-start.13 = (f32[2048]{0:T(1024)S(1)}, f32[2048]{0:T(1024)}, u32[]{:S(2)}) copy-start(f32[2048]{0:T(1024)} %param.14) | copy-start | bytes 24580
  13.4 4.5 %copy-start.14 = (u32[256]{0:T(256)S(1)}, u32[256]{0:T(256)}, u32[]{:S(2)}) copy-start(u32[256]{0:T(256)} %constant.98) | copy-start | bytes 3076
  14.6 312.7 %all-gather.5.cloned.1.call-start = ((), (), s32[]{:S(2)}) async-start(), calls=%async_computation.1 | async-start | bytes 8650752 | tf_op jit(solution)/shard_map/all_gather | solution.py:30
  88.3 10.8 %copy-start.2 = (bf16[32,128,128]{2,1,0:T(8,128)(2,1)}, bf16[32,128,128]{2,1,0:T(8,128)(2,1)S(1)}, u32[]{:S(2)}) copy-start(bf16[32,128,128]{2,1,0:T(8,128)(2,1)S(1)} %multiply_convert_fusion.1) | copy-start | bytes 3145732
  97.4 1.2 copy-start
  98.7 0.8 copy-start.7
  99.5 1.2 copy-start.6
  248.3 1.2 copy-start.1
  248.3 1.4 copy-start.8
  249.6 1.1 copy-start.4
  250.7 1.8 copy-start.11
  408.1 1.4 copy-start.10
  408.2 1.7 copy-start.9
  409.6 1.2 copy-start.3
  412.2 1.8 copy-start.5
Sparse Core Ops, SparseCore 0:
  14.8 80.4 all-gather.2
  104.6 133.7 all-gather.4
where the time goes:
time: 425 us; the launch traced here: 422 us
  blocking collectives  284 us (67%)
  other arithmetic  79.3 us (19%)
  local copies, waits for them, and re-layouts  25.1 us (6%)
  between operations  15.1 us (4%)
  matrix products  10.3 us (2%)
  waiting for transfers between devices  7.01 us (2%)
    unnamed x2, blocking collectives  211 us
    psum x1, blocking collectives, per_device(): lax.psum(gain_terms.reshape(H * E), ('dp', 'ctx')) / math.sqrt(total_tokens)  73.1 us
    add x31, other arithmetic, chain_join(): state_sum = later[0] + keep * earlier[0]  55.5 us
    sub x31, other arithmetic, chain_join(): keep = (1.0 - later[1]).reshape((-1,) + (1,) * (later[0].ndim - 1))  18.2 us
    unnamed x42, local copies, waits for them, and re-layouts  15.2 us
  transfers between devices with their start and end apart: 2, of which 1 were waited for; matrix products, arithmetic and copies ran while one was open for 2% of the time, Pallas kernels for 0%

commit v1 on v0

--- a/solution.py
+++ b/solution.py
@@ -167,7 +167,10 @@
     returned = results[:4]
     gain_terms = results[4]
     total_tokens = local_seqs * lax.axis_size("dp") * block_len * ctx_count
-    grad_gain = lax.psum(gain_terms.reshape(H * E), ("dp", "ctx")) / math.sqrt(total_tokens)
+    case_play = lambda own_rows: jnp.sum(
+        jax.lax.all_gather(own_rows, axis_name=("dp", "ctx")), axis=0
+    )
+    grad_gain = case_play(gain_terms.reshape(H * E)) / math.sqrt(total_tokens)
     flat = (local_seqs, block_len, H * E)
     outputs = tuple((item.reshape(flat) for item in returned))
     return (outputs[0], outputs[1], outputs[2], outputs[3], grad_gain)

time: 425 us -> 440 us (1.035)
  waiting for transfers between devices: 7.01 us -> 90.4 us
  blocking collectives: 284 us -> 211 us
    psum x1 -> x0, blocking collectives: 73.1 us -> none  [per_device(): lax.psum(gain_terms.reshape(H * E), ('dp', 'ctx')) / math.sqrt(total_tokens)]
    all_gather x1, waiting for transfers between devices: 0.01 us -> 56.4 us  [carried_in(): lax.all_gather(a.astype(kind), axis)]
    all_gather x0 -> x1, waiting for transfers between devices: none -> 27 us  [per_device(): jax.lax.all_gather(own_rows, axis_name=('dp', 'ctx'))]
    unnamed x42 -> x51, local copies, waits for them, and re-layouts: 15.2 us -> 16.9 us
  transfers between devices with their start and end apart: 2 -> 3, of which waited for: 1 -> 3; matrix products, arithmetic and copies ran while one was open for 2% -> 4% of each run, Pallas kernels for 0% -> 0%
where the time goes in v1:
time: 440 us; the launch traced here: 438 us
  blocking collectives  211 us (48%)
  waiting for transfers between devices  90.4 us (21%)
  other arithmetic  83.3 us (19%)
  local copies, waits for them, and re-layouts  26.7 us (6%)
  between operations  14.8 us (3%)
  matrix products  10.3 us (2%)
    unnamed x2, blocking collectives  211 us
    all_gather x1, waiting for transfers between devices, carried_in(): lax.all_gather(a.astype(kind), axis)  56.4 us
    add x31, other arithmetic, chain_join(): state_sum = later[0] + keep * earlier[0]  55.5 us
    all_gather x1, waiting for transfers between devices, per_device(): jax.lax.all_gather(own_rows, axis_name=('dp', 'ctx'))  27 us
    sub x31, other arithmetic, chain_join(): keep = (1.0 - later[1]).reshape((-1,) + (1,) * (later[0].ndim - 1))  18.2 us
    unnamed x51, local copies, waits for them, and re-layouts  16.9 us
  transfers between devices with their start and end apart: 3, of which 3 were waited for; matrix products, arithmetic and copies ran while one was open for 4% of the time, Pallas kernels for 0%

profile of v1, /device:TPU:32, one launch (start us, length us, event | category | flops | bytes accessed | tf_op | source)
XLA Modules:
  0.0 437.5 jit_solution(5215919654126572247)
XLA Ops:
  7.2 0.8 reduce_window_sum.22
  10.4 1.3 copy.66
  11.7 1.3 copy.67
  13.5 1.2 all_gather_reshape.6
  15.3 1.3 copy.65
  16.7 1.2 copy.70
  19.2 68.4 %all-reduce = f32[32]{0:T(128)S(1)} all-reduce(f32[32]{0:T(128)S(1)} %bitcast_dynamic-update-slice_fusion), channel_id=1, replica_groups=mesh['dp'=8,'ctx'=32] {'ctx'}, use_global_device_ids=true, to_apply=%add | all-reduce | flops 32 | bytes 256
  88.3 7.0 %all-gather.5.cloned.1.call-done = f32[32,1,32,4096]{3,2,1,0:T(8,128)} async-done(((f32[1,1,32,4096]{3,2,1,0:T(8,128)}), f32[32,1,32,4096]{3,2,1,0:T(8,128)}) %all-gather.5.cloned.1.call-update) | async-done | bytes 16777232 | tf_op jit(solution)/shard_map/all_gather | solution.py:14
  95.4 1.4 reshape.495
  97.7 1.1 copy-done
  98.8 0.8 copy-done.9
  100.0 0.8 multiply_reduce_fusion.2
  100.9 0.9 copy-done.6
  101.8 0.8 multiply_reduce_fusion
  103.4 2.5 divide_convert_fusion
  106.3 1.2 convert_element_type.251
  108.3 142.5 %all-reduce.1 = bf16[32]{0:T(256)(128)(2,1)S(1)} all-reduce(bf16[32]{0:T(256)(128)(2,1)S(1)} %dynamic-update-slice.1), channel_id=1, replica_groups=mesh['dp'=8,'ctx'=32] {'ctx'}, use_global_device_ids=true, to_apply=%add.1 | all-reduce | flops 32 | bytes 128
  253.1 0.8 fusion.13
  253.9 1.0 copy.76
  255.0 1.0 copy.75
  256.0 27.0 %all-gather.9.cloned.1.call-done = f32[256,1,2048]{2,1,0:T(1,128)} async-done(((f32[1,1,2048]{2,1,0:T(1,128)}), f32[256,1,2048]{2,1,0:T(1,128)}) %all-gather.9.cloned.1.call-update) | async-done | bytes 2097168 | tf_op jit(solution)/shard_map/all_gather | solution.py:171
  283.0 2.8 reduce_sum.62
  286.4 56.4 %all-gather.7.cloned.1.call-done = bf16[32,1,32,4096]{3,2,1,0:T(8,128)(2,1)} async-done(((bf16[1,1,32,4096]{3,2,1,0:T(8,128)(2,1)}), bf16[32,1,32,4096]{3,2,1,0:T(8,128)(2,1)}) %all-gather.7.cloned.1.call-update) | async-done | bytes 8388624 | tf_op jit(solution)/shard_map/all_gather | solution.py:30
  342.8 74.7 %while.27 = (s32[]{:T(128)}, f32[1,32,4096]{2,1,0:T(8,128)S(1)}, s32[]{:T(128)}, bf16[32,1,32,4096]{3,2,1,0:T(8,128)(2,1)}, bf16[32,1]{0,1:T(2,128)(2,1)S(1)}, /*index=5*/s32[]{:T(128)}, s32[]{:T(128)}, s32[]{:T(128)}, s32[]{:T(128)}) while((s32[]{:T(128)}, f32[1,32,4096]{2,1,0:T(8,128)S(1)}, s32[]{:T(128)}, ...), condition=%wide.region_9.10_spmd, body=%wide.region_8.9_spmd.sunk | while | flops 393223 | bytes 1310877 | solution.py:45
  343.4 1.8 convert_add_fusion.2
  345.8 1.8 convert_add_fusion.2
  348.2 1.8 convert_add_fusion.2
  350.6 1.8 convert_add_fusion.2
  353.0 1.8 convert_add_fusion.2
  355.4 1.8 convert_add_fusion.2
  357.8 1.8 convert_add_fusion.2
  360.2 1.8 convert_add_fusion.2
  362.6 1.8 convert_add_fusion.2
  365.0 1.8 convert_add_fusion.2
  367.4 1.8 convert_add_fusion.2
  369.9 1.8 convert_add_fusion.2
  372.3 1.8 convert_add_fusion.2
  374.7 1.8 convert_add_fusion.2
  377.1 1.8 convert_add_fusion.2
  379.5 1.8 convert_add_fusion.2
  381.9 1.8 convert_add_fusion.2
  384.3 1.8 convert_add_fusion.2
  386.7 1.8 convert_add_fusion.2
  389.1 1.8 convert_add_fusion.2
  391.5 1.8 convert_add_fusion.2
  393.9 1.8 convert_add_fusion.2
  396.3 1.8 convert_add_fusion.2
  398.7 1.8 convert_add_fusion.2
  401.1 1.8 convert_add_fusion.2
  403.5 1.8 convert_add_fusion.2
  405.9 1.8 convert_add_fusion.2
  408.3 1.8 convert_add_fusion.2
  410.7 1.8 convert_add_fusion.2
  413.1 1.8 convert_add_fusion.2
  415.5 1.8 convert_add_fusion.2
  417.5 1.5 reshape.500
  419.5 1.3 fusion.46
  420.8 1.3 fusion.45
  422.1 1.6 copy.72
  423.8 1.3 copy-done.14
  425.4 0.9 copy-done.3
  426.7 1.0 copy.78
  427.7 1.8 fusion.11
  430.0 1.0 copy.77
  (108 shorter events, 31.1 us)
Async XLA Ops:
  7.2 88.1 %all-gather.5.cloned.1.call-start = ((), (), s32[]{:S(2)}) async-start(), calls=%async_computation | async-start | bytes 17301504 | tf_op jit(solution)/shard_map/all_gather | solution.py:14
  13.4 3.2 copy-start.16
  13.4 4.5 %copy-start.17 = (f32[2048]{0:T(1024)S(1)}, f32[2048]{0:T(1024)}, u32[]{:S(2)}) copy-start(f32[2048]{0:T(1024)} %param.14) | copy-start | bytes 24580
  13.4 4.5 %copy-start.18 = (u32[256]{0:T(256)S(1)}, u32[256]{0:T(256)}, u32[]{:S(2)}) copy-start(u32[256]{0:T(256)} %constant.98) | copy-start | bytes 3076
  14.6 268.4 %all-gather.9.cloned.1.call-start = ((), (), s32[]{:S(2)}) async-start(), calls=%async_computation.2 | async-start | bytes 2105344 | tf_op jit(solution)/shard_map/all_gather | solution.py:171
  88.3 11.7 %copy-start.2 = (bf16[32,128,128]{2,1,0:T(8,128)(2,1)}, bf16[32,128,128]{2,1,0:T(8,128)(2,1)S(1)}, u32[]{:S(2)}) copy-start(bf16[32,128,128]{2,1,0:T(8,128)(2,1)S(1)} %multiply_convert_fusion.1) | copy-start | bytes 3145732
  97.3 2.7 copy-start.12
  97.3 1.4 copy-start
  98.8 0.8 copy-start.9
  100.0 1.8 copy-start.7
  100.9 1.0 copy-start.6
  100.9 2.6 copy-start.8
  103.4 239.4 %all-gather.7.cloned.1.call-start = ((), (), s32[]{:S(2)}) async-start(), calls=%async_computation.1 | async-start | bytes 8650752 | tf_op jit(solution)/shard_map/all_gather | solution.py:30
  105.9 144.9 %copy-start.13 = (bf16[32,64,64]{2,1,0:T(8,128)(2,1)S(1)}, bf16[32,64,64]{2,1,0:T(8,128)(2,1)}, u32[]{:S(2)}) copy-start(bf16[32,64,64]{2,1,0:T(8,128)(2,1)} %copy-done.12) | copy-start | bytes 786436
  250.8 1.2 copy-start.1
  250.8 1.4 copy-start.10
  252.1 1.0 copy-start.4
  253.1 1.8 copy-start.15
  423.7 1.4 copy-start.14
  423.8 1.7 copy-start.11
  425.1 1.2 copy-start.3
  427.7 1.8 copy-start.5
Sparse Core Ops, SparseCore 0:
  14.7 80.4 all-gather.4
  103.5 179.4 all-gather.8
  285.6 57.1 all-gather.6
